TPU v7x, 32 devices: a whole 2x2x4 slice. The times are simulated.
32 devices in a mesh: cell: 2 (over x), row: 8 (over z, y), col: 2 (over core).
Axes of the slice: x: 2, y: 2, z: 4, core: 2. Of those that a mesh axis runs over, the one named last changes fastest.
Arguments:
- half_system: bfloat16 [32768, 32768], P(('cell', 'row'), 'col'), parts along dimension 0, may hold values from -6 to 6
- vectors: bfloat16 [65536, 512], P(('cell', 'col', 'row')), parts along dimension 0, may hold values from -0.03125 to 0.03125
- edge: bfloat16 [512, 64, 512], P(('cell', 'row'), None, 'col'), parts along dimension 0, may hold values from -6 to 6
- ket: bfloat16 [128, 128], P('cell'), parts along dimension 0, may hold values from -0.5 to 0.5
- bra: bfloat16 [128, 128], P('cell'), parts along dimension 0, may hold values from -0.75 to 0.75
Outputs:
- new_edge: bfloat16 [1024, 64, 512], P(('cell', 'row'), None, 'col'), parts along dimension 0
There are 2 independent parts, one for each index of `cell`. A program takes and returns all parts, laid end to end along the dimension named above; each array names one. Nothing has to cross between parts.
All inputs are finite; a program needn't handle non-finite values.
Results may differ from a plain program's by a relative error of at most 0.0076.
Values may be sent and summed in bfloat16 or wider, within the bound.
A program may use at most 128 MiB of HBM per device.

v0:
```python
import jax
import jax.numpy as jnp
from jax import lax
from jax.sharding import PartitionSpec as P

D2 = 64
CL = 256


def per_device(half_system, vectors, edge, ket, bra):
    partial_value = jnp.dot(
        half_system,
        lax.all_gather(vectors, "row", axis=0, tiled=True),
        preferred_element_type=jnp.float32,
    )
    projector = lax.psum_scatter(partial_value, "col", scatter_dimension=1, tiled=True).astype(
        jnp.bfloat16
    )
    layer = jnp.dot(ket, bra.T, preferred_element_type=jnp.float32).astype(jnp.bfloat16)
    absorbed = jnp.einsum("aub,us->asb", edge, layer, preferred_element_type=jnp.float32).astype(
        jnp.bfloat16
    )
    left_count = edge.shape[0]
    proj3 = projector.reshape(left_count, D2, projector.shape[1])
    moved_proj, moved_edge = (
        lax.all_to_all(proj3, "row", split_axis=1, concat_axis=0, tiled=True),
        lax.all_to_all(absorbed, "row", split_axis=1, concat_axis=0, tiled=True),
    )
    moved_proj = lax.all_gather(moved_proj, "col", axis=2, tiled=True)
    middle = jnp.einsum("asc,asb->scb", moved_proj, moved_edge, preferred_element_type=jnp.float32)
    middle = (middle * CL ** (-0.5)).astype(jnp.bfloat16)
    regrouped = lax.all_to_all(middle, "row", split_axis=1, concat_axis=0, tiled=True)
    new_edge = jnp.einsum("ts,scb->ctb", layer, regrouped, preferred_element_type=jnp.float32)
    return new_edge.astype(jnp.bfloat16)


def solution(mesh):
    placed = (
        P(("cell", "row"), "col"),
        P(("cell", "col", "row"), None),
        P(("cell", "row"), None, "col"),
        P("cell", None),
        P("cell", None),
    )
    return jax.shard_map(
        per_device,
        mesh=mesh,
        in_specs=placed,
        out_specs=P(("cell", "row"), None, "col"),
        check_vma=False,
    )
```

profile of v0, /device:TPU:13, one launch (start us, length us, event | category | flops | bytes accessed | tf_op | source)
XLA Modules:
  0.0 420.7 jit_solution(11458914305922293366)
XLA Ops:
  6.5 0.0 copy-start
  6.5 0.0 all-gather.3.cloned.1.call-start
  6.5 0.7 all-gather.3.cloned.1.call-update
  7.3 0.0 reduce-scatter.2.cloned.1.call-start
  7.3 227.3 %all-gather.3.cloned.1.call-done = bf16[16384,512]{1,0:T(8,128)(2,1)} async-done(((bf16[2048,512]{1,0:T(8,128)(2,1)}), bf16[16384,512]{1,0:T(8,128)(2,1)}) %all-gather.3.cloned.1.call-update) | async-done | bytes 16777232 | tf_op jit(solution)/shard_map/all_gather | solution.py:13
  234.6 44.5 %fusion.7 = f32[2048,512]{1,0:T(8,128)} fusion(bf16[2048,16384]{1,0:T(8,128)(2,1)} %param.5, bf16[16384,512]{1,0:T(8,128)(2,1)} %all-gather.3.cloned.1.call-done), kind=kOutput, calls=%fused_computation.9 | convolution fusion | flops 34359738368 | bytes 88080384 | tf_op jit(solution)/shard_map/dot_general | solution.py:11
  279.1 0.0 reduce-scatter.2.cloned.1.call-update
  279.1 14.2 %reduce-scatter.2.cloned.1.call-done = f32[2048,256]{1,0:T(8,128)} async-done(((f32[2048,512]{1,0:T(8,128)}), f32[2048,256]{1,0:T(8,128)}) %reduce-scatter.2.cloned.1.call-update) | async-done | bytes 2097168 | tf_op jit(solution)/shard_map/reduce_scatter | solution.py:16
  293.3 1.7 convert_element_type.21
  295.0 0.0 copy-start.1
  295.0 0.0 copy-start.2
  295.1 1.6 copy.19
  296.6 5.5 %all-to-all-start = ((bf16[32,64,256]{2,0,1:T(8,128)(2,1)}), bf16[32,64,256]{2,0,1:T(8,128)(2,1)S(1)}, u32[]{:S(2)}, u32[]{:S(2)}) async-start(bf16[32,64,256]{2,0,1:T(8,128)(2,1)} %copy.19), calls=%async_computation.1 | async-start | bytes 2097152 | tf_op jit(solution)/shard_map/all_to_all | solution.py:26
  302.1 0.0 all-gather.5.cloned.1.call-start
  302.1 0.0 copy-done.1
  302.1 0.0 copy-done.2
  302.1 0.1 fusion.6
  302.2 23.1 %all-to-all-done = bf16[32,64,256]{2,0,1:T(8,128)(2,1)S(1)} async-done(((bf16[32,64,256]{2,0,1:T(8,128)(2,1)}), bf16[32,64,256]{2,0,1:T(8,128)(2,1)S(1)}, u32[]{:S(2)}, u32[]{:S(2)}) %all-to-all-start) | async-done | bytes 1048608 | tf_op jit(solution)/shard_map/all_to_all | solution.py:26
  325.3 0.6 copy.21
  326.0 1.6 copy.22
  327.5 0.0 all-gather.5.cloned.1.call-update
  327.5 0.0 copy-done
  327.6 0.4 fusion.5
  328.0 0.6 copy.24
  328.6 29.0 %all_to_all.54 = bf16[32,64,256]{2,0,1:T(8,128)(2,1)S(1)} all-to-all(bf16[32,64,256]{2,0,1:T(8,128)(2,1)S(1)} %copy.24), channel_id=1, replica_groups=mesh['cell'=2,'row'=8,'col'=2] {'row'}, dimensions={1} | all-to-all | bytes 2097152 | tf_op jit(solution)/shard_map/all_to_all | solution.py:27
  357.6 0.1 copy.25
  357.7 0.0 all-gather.5.cloned.1.call-done
  357.7 2.3 multiply_convert_fusion
  360.0 1.2 copy.26
  361.2 50.9 %all_to_all.55 = bf16[8,512,256]{2,0,1:T(8,128)(2,1)S(1)} all-to-all(bf16[8,512,256]{2,0,1:T(8,128)(2,1)S(1)} %copy.26), channel_id=1, replica_groups=mesh['cell'=2,'row'=8,'col'=2] {'row'}, dimensions={1} | all-to-all | bytes 4194304 | tf_op jit(solution)/shard_map/all_to_all | solution.py:32
  412.1 2.0 convert_bitcast_fusion
Async XLA Ops:
  6.5 321.0 %copy-start = (bf16[32,64,256]{2,1,0:T(8,128)(2,1)S(1)}, bf16[32,64,256]{2,1,0:T(8,128)(2,1)}, u32[]{:S(2)}) copy-start(bf16[32,64,256]{2,1,0:T(8,128)(2,1)} %param.7) | copy-start | bytes 3145732
  6.5 228.1 %all-gather.3.cloned.1.call-start = ((), (), s32[]{:S(2)}) async-start(), calls=%async_computation.4 | async-start | bytes 18874368 | tf_op jit(solution)/shard_map/all_gather | solution.py:13
  7.3 286.1 %reduce-scatter.2.cloned.1.call-start = ((), (), s32[]{:S(2)}) async-start(), calls=%async_computation.5 | async-start | bytes 6291456 | tf_op jit(solution)/shard_map/reduce_scatter | solution.py:16
  295.0 7.1 %copy-start.1 = (bf16[64,128]{1,0:T(8,128)(2,1)S(1)}, bf16[64,128]{1,0:T(8,128)(2,1)}, u32[]{:S(2)}) copy-start(bf16[64,128]{1,0:T(8,128)(2,1)} %param.8) | copy-start | bytes 49156
  295.0 7.1 %copy-start.2 = (bf16[64,128]{1,0:T(8,128)(2,1)S(1)}, bf16[64,128]{1,0:T(8,128)(2,1)}, u32[]{:S(2)}) copy-start(bf16[64,128]{1,0:T(8,128)(2,1)} %param.9) | copy-start | bytes 49156
  296.6 28.7 %all-to-all-start = ((bf16[32,64,256]{2,0,1:T(8,128)(2,1)}), bf16[32,64,256]{2,0,1:T(8,128)(2,1)S(1)}, u32[]{:S(2)}, u32[]{:S(2)}) async-start(bf16[32,64,256]{2,0,1:T(8,128)(2,1)} %copy.19), calls=%async_computation.1 | async-start | bytes 2097152 | tf_op jit(solution)/shard_map/all_to_all | solution.py:26
  302.1 55.6 %all-gather.5.cloned.1.call-start = ((), (), s32[]{:S(2)}) async-start(), calls=%async_computation.6 | async-start | bytes 3145728 | tf_op jit(solution)/shard_map/all_gather | solution.py:29
Sparse Core Ops, SparseCore 0:
  9.5 225.0 all-gather.2
  279.2 14.0 reduce-scatter.1
  327.7 12.8 all-gather.4
where the time goes:
time: 426 us; the launch traced here: 421 us
  waiting for transfers between devices  265 us (62%)
  blocking collectives  79.9 us (19%)
  matrix products  49.4 us (12%)
  between operations  13.2 us (3%)
  local copies, waits for them, and re-layouts  5.63 us (1%)
  starting transfers between devices  5.51 us (1%)
    all_gather x1, waiting for transfers between devices, per_device(): lax.all_gather(vectors, 'row', axis=0, tiled=True)  227 us
    all_to_all x1, blocking collectives, per_device(): lax.all_to_all(middle, 'row', split_axis=1, concat_axis=0, tiled=True)  50.9 us
    dot_general x1, matrix products, per_device(): jnp.dot(half_system, lax.all_gather(vectors, 'row', axis=0, tiled=True),...  44.5 us
    all_to_all x1, blocking collectives, per_device(): lax.all_to_all(absorbed, 'row', split_axis=1, concat_axis=0, tiled=True)  29 us
    all_to_all x1, waiting for transfers between devices, per_device(): lax.all_to_all(proj3, 'row', split_axis=1, concat_axis=0, tiled=True)  23.1 us
    reduce_scatter x1, waiting for transfers between devices, per_device(): lax.psum_scatter(partial_value, 'col', scatter_dimension=1, tiled=True)  14.2 us
  transfers between devices with their start and end apart: 4, of which 3 were waited for; matrix products, arithmetic and copies ran while one was open for 0% of the time, Pallas kernels for 0%

commit v1 on v0

v1 whole, which is shorter than its diff:
```python
import functools

import jax
import jax.numpy as jnp
from jax import lax
from jax.experimental import pallas as pl
from jax.experimental.pallas import tpu as pltpu
from jax.sharding import PartitionSpec as P

MESH = pl.DeviceIdType.MESH
SUBS = 2
GROUP = 2


def plain(half_system, vectors, edge, ket, bra):
    partial_value = jnp.dot(
        half_system,
        lax.all_gather(vectors, "row", axis=0, tiled=True),
        preferred_element_type=jnp.float32,
    )
    projector = lax.psum_scatter(partial_value, "col", scatter_dimension=1, tiled=True).astype(
        jnp.bfloat16
    )
    layer = jnp.dot(ket, bra.T, preferred_element_type=jnp.float32).astype(jnp.bfloat16)
    absorbed = jnp.einsum("aub,us->asb", edge, layer, preferred_element_type=jnp.float32).astype(
        jnp.bfloat16
    )
    left_count, d2 = edge.shape[0], edge.shape[1]
    proj3 = projector.reshape(left_count, d2, projector.shape[1])
    moved_proj, moved_edge = (
        lax.all_to_all(proj3, "row", split_axis=1, concat_axis=0, tiled=True),
        lax.all_to_all(absorbed, "row", split_axis=1, concat_axis=0, tiled=True),
    )
    moved_proj = lax.all_gather(moved_proj, "col", axis=2, tiled=True)
    middle = jnp.einsum("asc,asb->scb", moved_proj, moved_edge, preferred_element_type=jnp.float32)
    middle = (middle * moved_edge.shape[0] ** (-0.5)).astype(jnp.bfloat16)
    regrouped = lax.all_to_all(middle, "row", split_axis=1, concat_axis=0, tiled=True)
    new_edge = jnp.einsum("ts,scb->ctb", layer, regrouped, preferred_element_type=jnp.float32)
    return new_edge.astype(jnp.bfloat16)


def row_at(place, rows):
    half = rows // 2
    return jnp.where(place < half, place * 2, (rows - 1 - place) * 2 + 1)


def kernel(
    n, left, sblk, cblk, scale,
    half_ref, vec_ref, abs_ref, out_ref,
    vbuf, hbuf, acc, xbuf, psend, gbuf, abuf, msend,
    lsem, hsem, vsend, vrecv, asend, arecv, xsem, psem_s, psem_r, msem_s, msem_r,
):
    row, col = lax.axis_index("row"), lax.axis_index("col")
    other = 1 - col
    place = jnp.where(lax.rem(row, 2) == 0, row // 2, n - 1 - row // 2)
    ahead = row_at(lax.rem(place + 1, n), n)
    behind = row_at(lax.rem(place + n - 1, n), n)
    kb = vec_ref.shape[0]
    piece = kb // (2 * SUBS)
    per = 2 * SUBS
    d2 = n * sblk
    hrows = half_ref.shape[0]
    tile = min(512, hrows)

    barrier = pltpu.get_barrier_semaphore()
    for step in range(1, n):
        peer = lax.rem(row + step, n)
        for c in range(2):
            pl.semaphore_signal(barrier, inc=1, device_id={"row": peer, "col": c}, device_id_type=MESH)
    pl.semaphore_signal(barrier, inc=1, device_id={"col": other}, device_id_type=MESH)

    def own(d, sub):
        start = (d * SUBS + sub) * piece
        return pltpu.make_async_copy(vec_ref.at[pl.ds(start, piece), :], vbuf.at[row, d, sub], lsem.at[d, sub])

    for sub in range(SUBS):
        for d in range(2):
            own(d, sub).start()

    def owner(s, d):
        return row_at(lax.rem(place - s + n, n) if d == 0 else lax.rem(place + s, n), n)

    def hcopy(s, k):
        sub, d = k // 2, k % 2
        start = pl.multiple_of(owner(s, d) * kb + (d * SUBS + sub) * piece, piece)
        return pltpu.make_async_copy(half_ref.at[:, pl.ds(start, piece)], hbuf.at[k], hsem.at[k])

    for k in range(per):
        hcopy(0, k).start()
    acc[...] = jnp.zeros_like(acc)

    def vcopy(s, sub, d):
        slot = vbuf.at[owner(s, d), d, sub]
        return pltpu.make_async_remote_copy(
            src_ref=slot, dst_ref=slot, send_sem=vsend.at[d, s, sub], recv_sem=vrecv.at[d, s, sub],
            device_id={"row": ahead if d == 0 else behind}, device_id_type=MESH,
        )

    def varrival(s, sub, d):
        slot = vbuf.at[owner(s + 1, d), d, sub]
        return pltpu.make_async_remote_copy(
            src_ref=slot, dst_ref=slot, send_sem=vsend.at[d, s, sub], recv_sem=vrecv.at[d, s, sub],
            device_id={"row": ahead if d == 0 else behind}, device_id_type=MESH,
        )

    def acopy(step, source):
        peer = lax.rem(row + step, n)
        where = row if source else lax.rem(row + n - step, n)
        dst = abuf.at[col, :, pl.ds(pl.multiple_of(where * left, left), left), :]
        return pltpu.make_async_remote_copy(
            src_ref=abs_ref.at[peer], dst_ref=dst, send_sem=asend.at[step], recv_sem=arecv.at[step],
            device_id={"row": peer}, device_id_type=MESH,
        )

    def aown():
        dst = abuf.at[col, :, pl.ds(pl.multiple_of(row * left, left), left), :]
        return pltpu.make_async_copy(abs_ref.at[row], dst, arecv.at[0])

    def apair(which):
        return pltpu.make_async_remote_copy(
            src_ref=abuf.at[which], dst_ref=abuf.at[which], send_sem=asend.at[n], recv_sem=arecv.at[n],
            device_id={"col": other}, device_id_type=MESH,
        )

    for sub in range(SUBS):
        for d in range(2):
            own(d, sub).wait()
    pl.semaphore_wait(barrier, 2 * (n - 1) + 1)

    @pl.loop(0, n)
    def _(s):
        for sub in range(SUBS):
            for d in range(2):
                @pl.when(s > 0)
                def _():
                    varrival(s - 1, sub, d).wait_recv()

                @pl.when(s < n - 1)
                def _():
                    vcopy(s, sub, d).start()

            if sub == SUBS - 1:
                @pl.when(s == 0)
                def _():
                    aown().start()
                    for step in range(1, n):
                        acopy(step, True).start()

                @pl.when(s == n // 2)
                def _():
                    aown().wait()
                    for step in range(1, n):
                        acopy(step, False).wait_recv()
                    apair(col).start()

            for d in range(2):
                k = 2 * sub + d
                hcopy(s, k).wait()

                @pl.loop(0, hrows // tile)
                def _(i):
                    rows = pl.ds(pl.multiple_of(i * tile, tile), tile)
                    value = jnp.dot(
                        hbuf[k, rows, :], vbuf[owner(s, d), d, sub], preferred_element_type=jnp.float32
                    )
                    for lane in range(acc.shape[0]):
                        acc[lane, rows, :] += value[:, lane * 128:(lane + 1) * 128]

                @pl.when(s < n - 1)
                def _():
                    hcopy(s + 1, k).start()

    lanes = acc.shape[0] // 2
    pair = pltpu.make_async_remote_copy(
        src_ref=acc.at[pl.ds(other * lanes, lanes)], dst_ref=xbuf, send_sem=xsem.at[0], recv_sem=xsem.at[1],
        device_id={"col": other}, device_id_type=MESH,
    )
    pair.start()
    pair.wait_recv()

    def pcopy(step, source):
        peer = lax.rem(row + step, n)
        where = row if source else lax.rem(row + n - step, n)
        dst = gbuf.at[:, pl.ds(pl.multiple_of(where * left, left), left), :]
        return pltpu.make_async_remote_copy(
            src_ref=psend.at[peer], dst_ref=dst, send_sem=psem_s.at[step], recv_sem=psem_r.at[step],
            device_id={"row": peer}, device_id_type=MESH,
        )

    def pown():
        dst = gbuf.at[:, pl.ds(pl.multiple_of(row * left, left), left), :]
        return pltpu.make_async_copy(psend.at[row], dst, psem_r.at[0])

    for step in list(range(1, n)) + [0]:
        peer = lax.rem(row + step, n)

        @pl.loop(0, sblk)
        def _(j):
            rows = pl.ds(peer * sblk + j, left, stride=d2)
            for lane in range(lanes):
                value = acc[col * lanes + lane, rows, :] + xbuf[lane, rows, :]
                psend[peer, j, :, lane * 128:(lane + 1) * 128] = value.astype(jnp.bfloat16)

        if step > 0:
            pcopy(step, True).start()
        else:
            pown().start()

    pown().wait()
    for step in range(1, n):
        pcopy(step, False).wait_recv()
    apair(other).wait_recv()

    rows_half = n // 2

    def mcopy(g, j, h):
        return pltpu.make_async_remote_copy(
            src_ref=msend.at[h, pl.ds(g * GROUP, GROUP), pl.ds(j * cblk, cblk), :],
            dst_ref=out_ref.at[pl.ds(row * sblk + g * GROUP, GROUP), :, :],
            send_sem=msem_s.at[g, j, h], recv_sem=msem_r.at[g, row],
            device_id={"row": col * rows_half + j, "col": h}, device_id_type=MESH,
        )

    def mown(g, j, h):
        return pltpu.make_async_copy(
            msend.at[h, pl.ds(g * GROUP, GROUP), pl.ds(j * cblk, cblk), :],
            out_ref.at[pl.ds(row * sblk + g * GROUP, GROUP), :, :],
            msem_s.at[g, j, h],
        )

    def is_self(j, h):
        return jnp.logical_and(col * rows_half + j == row, col == h)

    groups = sblk // GROUP
    for g in range(groups):
        for e in range(GROUP):
            at = g * GROUP + e
            for h in range(2):
                value = lax.dot_general(
                    gbuf[at], abuf[h, at], (((0,), (0,)), ((), ())), preferred_element_type=jnp.float32
                )
                msend[h, at] = (value * scale).astype(jnp.bfloat16)
        for j in range(rows_half):
            for h in range(2):
                same = is_self(j, h)

                @pl.when(same)
                def _():
                    mown(g, j, h).start()

                @pl.when(jnp.logical_not(same))
                def _():
                    mcopy(g, j, h).start()

    from_col = row // rows_half
    for g in range(groups):
        for q in range(n):
            @pl.when(jnp.logical_not(jnp.logical_and(row == q, from_col == col)))
            def _():
                dst = out_ref.at[pl.ds(q * sblk + g * GROUP, GROUP), :, :]
                pltpu.make_async_remote_copy(
                    src_ref=dst, dst_ref=dst, send_sem=msem_s.at[g, 0, 0], recv_sem=msem_r.at[g, q],
                    device_id={"col": other}, device_id_type=MESH,
                ).wait_recv()
        for j in range(rows_half):
            for h in range(2):
                same = is_self(j, h)

                @pl.when(same)
                def _():
                    mown(g, j, h).wait()

                @pl.when(jnp.logical_not(same))
                def _():
                    mcopy(g, j, h).wait_send()

    @pl.loop(0, n - 1)
    def _(s):
        for sub in range(SUBS):
            for d in range(2):
                vcopy(s, sub, d).wait_send()

    for step in range(1, n):
        acopy(step, True).wait_send()
        pcopy(step, True).wait_send()
    apair(col).wait_send()
    pair.wait_send()


def per_device(half_system, vectors, edge, ket, bra):
    n = lax.axis_size("row")
    left, d2, right = edge.shape
    kb, width = vectors.shape
    sblk, cblk = d2 // n, width // n
    fits = (
        lax.axis_size("col") == 2 and n % 2 == 0 and d2 % n == 0 and width % n == 0
        and left % 16 == 0 and cblk % 16 == 0 and sblk % GROUP == 0 and kb % (256 * SUBS) == 0
        and width % 256 == 0 and right % 128 == 0
    )
    if not fits:
        return plain(half_system, vectors, edge, ket, bra)
    bf16, f32 = jnp.bfloat16, jnp.float32
    layer = jnp.dot(ket, bra.T, preferred_element_type=f32).astype(bf16)
    absorbed = jnp.einsum("aub,us->sab", edge, layer, preferred_element_type=f32).astype(bf16)
    absorbed = absorbed.reshape(n, sblk, left, right)
    hrows, cols = half_system.shape
    piece = kb // (2 * SUBS)
    half = width // 2
    lanes = half // 128
    any_space = pl.BlockSpec(memory_space=pl.ANY)
    dma = pltpu.SemaphoreType.DMA
    regrouped = pl.pallas_call(
        functools.partial(kernel, n, left, sblk, cblk, float((n * left) ** -0.5)),
        out_shape=jax.ShapeDtypeStruct((d2, cblk, right), bf16),
        in_specs=[any_space] * 3,
        out_specs=any_space,
        scratch_shapes=[
            pltpu.VMEM((n, 2, SUBS, piece, width), bf16),
            pltpu.VMEM((2 * SUBS, hrows, piece), bf16),
            pltpu.VMEM((2 * lanes, hrows, 128), f32),
            pltpu.VMEM((lanes, hrows, 128), f32),
            pltpu.VMEM((n, sblk, left, half), bf16),
            pltpu.VMEM((sblk, n * left, half), bf16),
            pltpu.VMEM((2, sblk, n * left, right), bf16),
            pltpu.VMEM((2, sblk, half, right), bf16),
            dma((2, SUBS)),
            dma((2 * SUBS,)),
            dma((2, n - 1, SUBS)),
            dma((2, n - 1, SUBS)),
            dma((n + 1,)),
            dma((n + 1,)),
            dma((2,)),
            dma((n,)),
            dma((n,)),
            dma((sblk // GROUP, n // 2, 2)),
            dma((sblk // GROUP, n)),
        ],
        compiler_params=pltpu.CompilerParams(
            collective_id=0, has_side_effects=True, vmem_limit_bytes=60 * 1024 * 1024
        ),
        name="renormalize",
    )(half_system, vectors, absorbed)
    new_edge = jnp.einsum("ts,scb->ctb", layer, regrouped, preferred_element_type=f32)
    return new_edge.astype(bf16)


def solution(mesh):
    placed = (
        P(("cell", "row"), "col"),
        P(("cell", "col", "row"), None),
        P(("cell", "row"), None, "col"),
        P("cell", None),
        P("cell", None),
    )
    return jax.shard_map(
        per_device,
        mesh=mesh,
        in_specs=placed,
        out_specs=P(("cell", "row"), None, "col"),
        check_vma=False,
    )
```

time: 426 us -> 275 us (0.65); the launches traced: 421 us -> 275 us
  Pallas kernels: 0 us -> 267 us
  waiting for transfers between devices: 265 us -> 0 us
  blocking collectives: 79.9 us -> 0 us
  matrix products: 49.4 us -> 6.02 us
  between operations: 13.2 us -> 0.02 us
  starting transfers between devices: 5.51 us -> 0 us
    pallas_call x0 -> x1, Pallas kernels: none -> 267 us  [per_device(): pl.pallas_call(functools.partial(kernel, n, left, sblk, cblk, float((n *...]
    all_gather x2 -> x0, waiting for transfers between devices: 227 us -> none  [the longest x1 227 us: per_device(): lax.all_gather(vectors, 'row', axis=0, tiled=True)]
    all_to_all x2 -> x0, blocking collectives: 79.9 us -> none  [the longest x1 50.9 us: per_device(): lax.all_to_all(middle, 'row', split_axis=1, concat_axis=0, tiled=True)]
    dot_general x5 -> x3, matrix products: 49.4 us -> 6.02 us  [the longest x1 4.62 us: per_device(): jnp.einsum('ts,scb->ctb', layer, regrouped, preferred_element_type=f32)]
    all_to_all x1 -> x0, waiting for transfers between devices: 23.1 us -> none  [per_device(): lax.all_to_all(proj3, 'row', split_axis=1, concat_axis=0, tiled=True)]
    reduce_scatter x1 -> x0, waiting for transfers between devices: 14.2 us -> none  [per_device(): lax.psum_scatter(partial_value, 'col', scatter_dimension=1, tiled=True)]
    all_to_all x1 -> x0, starting transfers between devices: 5.47 us -> none  [per_device(): lax.all_to_all(proj3, 'row', split_axis=1, concat_axis=0, tiled=True)]
  transfers between devices with their start and end apart: 4 -> 0, of which waited for: 3 -> 0; matrix products, arithmetic and copies ran while one was open for 0% -> 0% of each run, Pallas kernels for 0% -> 0%
where the time goes in v1:
time: 275 us
  Pallas kernels  267 us (97%)
  matrix products  6.02 us (2%)
    pallas_call x1, Pallas kernels, per_device(): pl.pallas_call(functools.partial(kernel, n, left, sblk, cblk, float((n *...  267 us

profile of v1, /device:TPU:13, one launch (start us, length us, event | category | flops | bytes accessed | tf_op | source)
XLA Modules:
  0.0 275.1 jit_solution(1391724587175213566)
XLA Ops:
  0.0 0.0 copy-start
  0.0 0.9 fusion.4
  0.9 0.3 copy-done
  1.3 0.5 convolution_convert_fusion
  1.7 1.6 copy.7
  3.3 267.2 %renormalize.1 = bf16[64,64,256]{2,1,0:T(8,128)(2,1)} custom-call(bf16[2048,16384]{1,0:T(8,128)(2,1)} %half_ref.1, bf16[2048,512]{1,0:T(8,128)(2,1)} %vec_ref.1, bf16[8,8,32,256]{3,2,1,0:T(8,128)(2,1)} %bitcast.11), custom_call_target="tpu_custom_call" | custom-call | tf_op jit(solution)/shard_map/renormalize/pallas_call | solution.py:312
  270.5 4.6 %convert_bitcast_fusion = bf16[64,64,256]{2,1,0:T(8,128)(2,1)} fusion(bf16[64,64,1]{1,0,2:T(8,128)(2,1)S(1)} %fusion.4, bf16[64,64,256]{2,1,0:T(8,128)(2,1)} %renormalize.1), kind=kOutput, calls=%fused_computation.2 | convolution fusion | flops 135266304 | bytes 4202496 | tf_op jit(solution)/shard_map/ts,scb->ctb/dot_general | solution.py:343
Async XLA Ops:
  0.0 1.3 copy-start

commit v2 on v0

v2 whole, which is shorter than its diff:
```python
import functools

import jax
import jax.numpy as jnp
from jax import lax
from jax.experimental import pallas as pl
from jax.experimental.pallas import tpu as pltpu
from jax.sharding import PartitionSpec as P

MESH = pl.DeviceIdType.MESH
CHUNKS = 2
GROUP = 4


def plain(half_system, vectors, edge, ket, bra):
    partial_value = jnp.dot(
        half_system,
        lax.all_gather(vectors, "row", axis=0, tiled=True),
        preferred_element_type=jnp.float32,
    )
    projector = lax.psum_scatter(partial_value, "col", scatter_dimension=1, tiled=True).astype(
        jnp.bfloat16
    )
    layer = jnp.dot(ket, bra.T, preferred_element_type=jnp.float32).astype(jnp.bfloat16)
    absorbed = jnp.einsum("aub,us->asb", edge, layer, preferred_element_type=jnp.float32).astype(
        jnp.bfloat16
    )
    left_count, d2 = edge.shape[0], edge.shape[1]
    proj3 = projector.reshape(left_count, d2, projector.shape[1])
    moved_proj, moved_edge = (
        lax.all_to_all(proj3, "row", split_axis=1, concat_axis=0, tiled=True),
        lax.all_to_all(absorbed, "row", split_axis=1, concat_axis=0, tiled=True),
    )
    moved_proj = lax.all_gather(moved_proj, "col", axis=2, tiled=True)
    middle = jnp.einsum("asc,asb->scb", moved_proj, moved_edge, preferred_element_type=jnp.float32)
    middle = (middle * moved_edge.shape[0] ** (-0.5)).astype(jnp.bfloat16)
    regrouped = lax.all_to_all(middle, "row", split_axis=1, concat_axis=0, tiled=True)
    new_edge = jnp.einsum("ts,scb->ctb", layer, regrouped, preferred_element_type=jnp.float32)
    return new_edge.astype(jnp.bfloat16)


def kernel(
    n, left, sblk, cblk, scale,
    half_ref, vec_ref, abs_ref, out_ref,
    vbuf, hbuf, acc, xbuf, psend, gbuf, abuf, msend,
    lsem, hsem, vsend, vrecv, asend, arecv, xsem_s, xsem_r, psem_s, psem_r, msem_s, msem_r,
):
    row, col = lax.axis_index("row"), lax.axis_index("col")
    other = 1 - col
    z, y = row // 2, lax.rem(row, 2)
    far = n // 2
    kb = vec_ref.shape[0]
    ka = kb * 13 // 16
    d2 = n * sblk
    hrows = half_ref.shape[0]
    tile = min(256, hrows)
    visits = CHUNKS * far

    def zat(i):
        found = 0
        for zz in range(far):
            for at, value in enumerate(sorted(range(far), key=lambda w: abs(w - zz))):
                found = found + jnp.where(jnp.logical_and(z == zz, i == at), value, 0)
        return found

    barrier = pltpu.get_barrier_semaphore()
    for step in range(1, n):
        peer = lax.rem(row + step, n)
        for c in range(2):
            pl.semaphore_signal(barrier, inc=1, device_id={"row": peer, "col": c}, device_id_type=MESH)
    pl.semaphore_signal(barrier, inc=1, device_id={"col": other}, device_id_type=MESH)

    def lane_of(q, c):
        return 3 * c if q == 0 else 1 + c

    def own(q, c):
        return pltpu.make_async_copy(
            vec_ref.at[:, pl.ds(lane_of(q, c) * 128, 128)],
            vbuf.at[q, row, :, pl.ds(c * 128, 128)],
            lsem.at[q, c],
        )

    for q in range(CHUNKS):
        for c in range(2):
            own(q, c).start()

    def hcopy(v, yy, k):
        start = pl.multiple_of((zat(lax.rem(v, far)) * 2 + yy) * kb, kb)
        return pltpu.make_async_copy(half_ref.at[:, pl.ds(start, kb)], hbuf.at[k], hsem.at[k])

    hcopy(0, y, 0).start()
    hcopy(0, 1 - y, 1).start()
    acc[...] = jnp.zeros_like(acc)

    def vcopy(q, zi, yy, part, way):
        r = zi * 2 + yy
        slot = vbuf.at[q, r, pl.ds(0, ka) if part == 0 else pl.ds(ka, kb - ka), :]
        peer = (z + 1) * 2 + y if way == 0 else (z - 1) * 2 + y if way == 1 else z * 2 + 1 - y
        return pltpu.make_async_remote_copy(
            src_ref=slot, dst_ref=slot, send_sem=vsend.at[q, r, part, way], recv_sem=vrecv.at[q, r, part],
            device_id={"row": peer}, device_id_type=MESH,
        )

    def each_way(zi, mine, part, first, do):
        @pl.when(jnp.logical_and(zi <= z, z < far - 1))
        def _():
            do(0)

        @pl.when(jnp.logical_and(zi >= z, z > 0))
        def _():
            do(1)

        if mine and part == 0:
            do(2)
        if mine and part == 1:
            @pl.when(first)
            def _():
                do(2)

    def acopy(step, source):
        peer = lax.rem(row + step, n)
        where = row if source else lax.rem(row + n - step, n)
        dst = abuf.at[col, :, pl.ds(pl.multiple_of(where * left, left), left), :]
        return pltpu.make_async_remote_copy(
            src_ref=abs_ref.at[peer], dst_ref=dst, send_sem=asend.at[step], recv_sem=arecv.at[step],
            device_id={"row": peer}, device_id_type=MESH,
        )

    def aown():
        dst = abuf.at[col, :, pl.ds(pl.multiple_of(row * left, left), left), :]
        return pltpu.make_async_copy(abs_ref.at[row], dst, arecv.at[0])

    def apair(which):
        return pltpu.make_async_remote_copy(
            src_ref=abuf.at[which], dst_ref=abuf.at[which], send_sem=asend.at[n], recv_sem=arecv.at[n],
            device_id={"col": other}, device_id_type=MESH,
        )

    def multiply(v, yy, k):
        q = v // far
        r = zat(lax.rem(v, far)) * 2 + yy
        hcopy(v, yy, k).wait()

        @pl.loop(0, hrows // tile)
        def _(i):
            rows = pl.ds(pl.multiple_of(i * tile, tile), tile)
            value = jnp.dot(hbuf[k, rows, :], vbuf[q, r], preferred_element_type=jnp.float32)
            for lane in range(2):
                acc[q, lane, rows, :] += value[:, lane * 128:(lane + 1) * 128]

    def pair(q):
        return pltpu.make_async_remote_copy(
            src_ref=acc.at[q, other], dst_ref=xbuf.at[q], send_sem=xsem_s.at[q], recv_sem=xsem_r.at[q],
            device_id={"col": other}, device_id_type=MESH,
        )

    def pcopy(q, step, source):
        peer = lax.rem(row + step, n)
        where = row if source else lax.rem(row + n - step, n)
        dst = gbuf.at[q, :, pl.ds(pl.multiple_of(where * left, left), left), :]
        return pltpu.make_async_remote_copy(
            src_ref=psend.at[q, peer], dst_ref=dst, send_sem=psem_s.at[q, step], recv_sem=psem_r.at[q, step],
            device_id={"row": peer}, device_id_type=MESH,
        )

    def pown(q):
        dst = gbuf.at[q, :, pl.ds(pl.multiple_of(row * left, left), left), :]
        return pltpu.make_async_copy(psend.at[q, row], dst, psem_r.at[q, 0])

    def project(q):
        pair(q).start()
        pair(q).wait_recv()
        mine = acc.at[q, col]
        theirs = xbuf.at[q]

        @pl.loop(0, n)
        def _(at):
            peer = lax.rem(row + 1 + at, n)

            @pl.loop(0, sblk)
            def _(j):
                rows = pl.ds(peer * sblk + j, left, stride=d2)
                psend[q, peer, j] = (mine[rows, :] + theirs[rows, :]).astype(jnp.bfloat16)

        for step in range(1, n):
            pcopy(q, step, True).start()
        pown(q).start()

    def mcopy(q, g, j, h):
        return pltpu.make_async_remote_copy(
            src_ref=msend.at[q, h, pl.ds(g * GROUP, GROUP), pl.ds(j * cblk, cblk), :],
            dst_ref=out_ref.at[pl.ds(row * sblk + g * GROUP, GROUP), :, :],
            send_sem=msem_s.at[q, g, j, h], recv_sem=msem_r.at[g, row],
            device_id={"row": lane_of(q, col) * 2 + j, "col": h}, device_id_type=MESH,
        )

    def mown(q, g, j, h):
        return pltpu.make_async_copy(
            msend.at[q, h, pl.ds(g * GROUP, GROUP), pl.ds(j * cblk, cblk), :],
            out_ref.at[pl.ds(row * sblk + g * GROUP, GROUP), :, :],
            msem_s.at[q, g, j, h],
        )

    groups = sblk // GROUP

    def every(q, g, local, remote):
        for j in range(2):
            for h in range(2):
                same = jnp.logical_and(lane_of(q, col) * 2 + j == row, col == h)

                @pl.when(same)
                def _():
                    local(mown(q, g, j, h))

                @pl.when(jnp.logical_not(same))
                def _():
                    remote(mcopy(q, g, j, h))

    def renormalize(q):
        pown(q).wait()
        for step in range(1, n):
            pcopy(q, step, False).wait_recv()
        if q == 0:
            apair(other).wait_recv()
        for g in range(groups):
            for e in range(GROUP):
                at = g * GROUP + e
                for h in range(2):
                    value = lax.dot_general(
                        gbuf[q, at], abuf[h, at], (((0,), (0,)), ((), ())),
                        preferred_element_type=jnp.float32,
                    )
                    msend[q, h, at] = (value * scale).astype(jnp.bfloat16)
            every(q, g, lambda copy: copy.start(), lambda copy: copy.start())

    for q in range(CHUNKS):
        for c in range(2):
            own(q, c).wait()
    pl.semaphore_wait(barrier, 2 * (n - 1) + 1)

    def take(v, mine, part):
        q, i = v // far, lax.rem(v, far)
        zi = zat(i)
        yy = y if mine else 1 - y

        def wait():
            vcopy(q, zi, yy, part, 2).wait_recv()

        if mine:
            pl.when(i > 0)(wait)
        else:
            wait()
        if mine or part == 1:
            each_way(zi, mine, part, i == 0, lambda way: vcopy(q, zi, yy, part, way).start())

    @pl.loop(0, visits)
    def _(v):
        take(v, True, 0)
        take(v, True, 1)

        @pl.when(v == 0)
        def _():
            aown().start()
            for step in range(1, n):
                acopy(step, True).start()

        multiply(v, y, 0)

        @pl.when(v < visits - 1)
        def _():
            hcopy(v + 1, y, 0).start()

        take(v, False, 1)

        @pl.when(v > 0)
        def _():
            take(v - 1, False, 0)
            multiply(v - 1, 1 - y, 1)
            hcopy(v, 1 - y, 1).start()

        @pl.when(v == 2)
        def _():
            aown().wait()
            for step in range(1, n):
                acopy(step, False).wait_recv()
            apair(col).start()

        @pl.when(v == far)
        def _():
            project(0)

        @pl.when(v == far + 1)
        def _():
            renormalize(0)

    take(visits - 1, False, 0)
    multiply(visits - 1, 1 - y, 1)
    project(1)
    renormalize(1)

    from_col = row // (n // 2)
    for g in range(groups):
        for w in range(n):
            @pl.when(jnp.logical_not(jnp.logical_and(row == w, from_col == col)))
            def _():
                dst = out_ref.at[pl.ds(w * sblk + g * GROUP, GROUP), :, :]
                pltpu.make_async_remote_copy(
                    src_ref=dst, dst_ref=dst, send_sem=msem_s.at[0, g, 0, 0], recv_sem=msem_r.at[g, w],
                    device_id={"col": other}, device_id_type=MESH,
                ).wait_recv()
        for q in range(CHUNKS):
            every(q, g, lambda copy: copy.wait(), lambda copy: copy.wait_send())

    @pl.loop(0, visits)
    def _(v):
        q, i = v // far, lax.rem(v, far)
        zi = zat(i)
        for mine, part in ((True, 0), (True, 1), (False, 1)):
            yy = y if mine else 1 - y
            each_way(zi, mine, part, i == 0, lambda way: vcopy(q, zi, yy, part, way).wait_send())

    for step in range(1, n):
        acopy(step, True).wait_send()
        for q in range(CHUNKS):
            pcopy(q, step, True).wait_send()
    apair(col).wait_send()
    for q in range(CHUNKS):
        pair(q).wait_send()


def per_device(half_system, vectors, edge, ket, bra):
    n = lax.axis_size("row")
    left, d2, right = edge.shape
    kb, width = vectors.shape
    sblk, cblk = d2 // n, width // n
    fits = (
        lax.axis_size("col") == 2 and n == 8 and d2 % n == 0 and width == 512
        and left % 16 == 0 and sblk % GROUP == 0 and kb % 256 == 0 and right % 128 == 0
    )
    if not fits:
        return plain(half_system, vectors, edge, ket, bra)
    bf16, f32 = jnp.bfloat16, jnp.float32
    layer = jnp.dot(ket, bra.T, preferred_element_type=f32).astype(bf16)
    absorbed = jnp.einsum("aub,us->sab", edge, layer, preferred_element_type=f32).astype(bf16)
    absorbed = absorbed.reshape(n, sblk, left, right)
    hrows, cols = half_system.shape
    half = width // 4
    any_space = pl.BlockSpec(memory_space=pl.ANY)
    dma = pltpu.SemaphoreType.DMA
    regrouped = pl.pallas_call(
        functools.partial(kernel, n, left, sblk, cblk, float((n * left) ** -0.5)),
        out_shape=jax.ShapeDtypeStruct((d2, cblk, right), bf16),
        in_specs=[any_space] * 3,
        out_specs=any_space,
        scratch_shapes=[
            pltpu.VMEM((CHUNKS, n, kb, 2 * half), bf16),
            pltpu.VMEM((2, hrows, kb), bf16),
            pltpu.VMEM((CHUNKS, 2, hrows, half), f32),
            pltpu.VMEM((CHUNKS, hrows, half), f32),
            pltpu.VMEM((CHUNKS, n, sblk, left, half), bf16),
            pltpu.VMEM((CHUNKS, sblk, n * left, half), bf16),
            pltpu.VMEM((2, sblk, n * left, right), bf16),
            pltpu.VMEM((CHUNKS, 2, sblk, half, right), bf16),
            dma((CHUNKS, 2)),
            dma((2,)),
            dma((CHUNKS, n, 2, 3)),
            dma((CHUNKS, n, 2)),
            dma((n + 1,)),
            dma((n + 1,)),
            dma((CHUNKS,)),
            dma((CHUNKS,)),
            dma((CHUNKS, n)),
            dma((CHUNKS, n)),
            dma((CHUNKS, sblk // GROUP, 2, 2)),
            dma((sblk // GROUP, n)),
        ],
        compiler_params=pltpu.CompilerParams(
            collective_id=0, has_side_effects=True, vmem_limit_bytes=60 * 1024 * 1024
        ),
        name="renormalize",
    )(half_system, vectors, absorbed)
    new_edge = jnp.einsum("ts,scb->ctb", layer, regrouped, preferred_element_type=f32)
    return new_edge.astype(bf16)


def solution(mesh):
    placed = (
        P(("cell", "row"), "col"),
        P(("cell", "col", "row"), None),
        P(("cell", "row"), None, "col"),
        P("cell", None),
        P("cell", None),
    )
    return jax.shard_map(
        per_device,
        mesh=mesh,
        in_specs=placed,
        out_specs=P(("cell", "row"), None, "col"),
        check_vma=False,
    )
```

time: 426 us -> 310 us (0.73); the launches traced: 421 us -> 310 us
  Pallas kernels: 0 us -> 302 us
  waiting for transfers between devices: 265 us -> 0 us
  blocking collectives: 79.9 us -> 0 us
  matrix products: 49.4 us -> 6.02 us
  between operations: 13.2 us -> 0.02 us
  starting transfers between devices: 5.51 us -> 0 us
    pallas_call x0 -> x1, Pallas kernels: none -> 302 us  [per_device(): pl.pallas_call(functools.partial(kernel, n, left, sblk, cblk, float((n *...]
    all_gather x2 -> x0, waiting for transfers between devices: 227 us -> none  [the longest x1 227 us: per_device(): lax.all_gather(vectors, 'row', axis=0, tiled=True)]
    all_to_all x2 -> x0, blocking collectives: 79.9 us -> none  [the longest x1 50.9 us: per_device(): lax.all_to_all(middle, 'row', split_axis=1, concat_axis=0, tiled=True)]
    dot_general x5 -> x3, matrix products: 49.4 us -> 6.02 us  [the longest x1 4.62 us: per_device(): jnp.einsum('ts,scb->ctb', layer, regrouped, preferred_element_type=f32)]
    all_to_all x1 -> x0, waiting for transfers between devices: 23.1 us -> none  [per_device(): lax.all_to_all(proj3, 'row', split_axis=1, concat_axis=0, tiled=True)]
    reduce_scatter x1 -> x0, waiting for transfers between devices: 14.2 us -> none  [per_device(): lax.psum_scatter(partial_value, 'col', scatter_dimension=1, tiled=True)]
    all_to_all x1 -> x0, starting transfers between devices: 5.47 us -> none  [per_device(): lax.all_to_all(proj3, 'row', split_axis=1, concat_axis=0, tiled=True)]
  transfers between devices with their start and end apart: 4 -> 0, of which waited for: 3 -> 0; matrix products, arithmetic and copies ran while one was open for 0% -> 0% of each run, Pallas kernels for 0% -> 0%
where the time goes in v2:
time: 310 us
  Pallas kernels  302 us (97%)
  matrix products  6.02 us (2%)
    pallas_call x1, Pallas kernels, per_device(): pl.pallas_call(functools.partial(kernel, n, left, sblk, cblk, float((n *...  302 us

profile of v2, /device:TPU:13, one launch (start us, length us, event | category | flops | bytes accessed | tf_op | source)
XLA Modules:
  0.0 309.8 jit_solution(14952218415119505937)
XLA Ops:
  0.0 0.0 copy-start
  0.0 0.9 fusion.4
  0.9 0.3 copy-done
  1.3 0.5 convolution_convert_fusion
  1.7 1.6 copy.7
  3.3 301.9 %renormalize.1 = bf16[64,64,256]{2,1,0:T(8,128)(2,1)} custom-call(bf16[2048,16384]{1,0:T(8,128)(2,1)} %half_ref.1, bf16[2048,512]{1,0:T(8,128)(2,1)} %vec_ref.1, bf16[8,8,32,256]{3,2,1,0:T(8,128)(2,1)} %bitcast.11), custom_call_target="tpu_custom_call" | custom-call | tf_op jit(solution)/shard_map/renormalize/pallas_call | solution.py:350
  305.1 4.6 %convert_bitcast_fusion = bf16[64,64,256]{2,1,0:T(8,128)(2,1)} fusion(bf16[64,64,1]{1,0,2:T(8,128)(2,1)S(1)} %fusion.4, bf16[64,64,256]{2,1,0:T(8,128)(2,1)} %renormalize.1), kind=kOutput, calls=%fused_computation.2 | convolution fusion | flops 135266304 | bytes 4202496 | tf_op jit(solution)/shard_map/ts,scb->ctb/dot_general | solution.py:382
Async XLA Ops:
  0.0 1.3 copy-start

commit v3 on v1

--- a/solution.py
+++ b/solution.py
@@ -9,7 +9,7 @@
 
 MESH = pl.DeviceIdType.MESH
 SUBS = 2
-GROUP = 2
+GROUP = 4
 
 
 def plain(half_system, vectors, edge, ket, bra):
@@ -171,44 +171,46 @@
                     hcopy(s + 1, k).start()
 
     lanes = acc.shape[0] // 2
-    pair = pltpu.make_async_remote_copy(
-        src_ref=acc.at[pl.ds(other * lanes, lanes)], dst_ref=xbuf, send_sem=xsem.at[0], recv_sem=xsem.at[1],
-        device_id={"col": other}, device_id_type=MESH,
-    )
-    pair.start()
-    pair.wait_recv()
-
-    def pcopy(step, source):
+
+    def pair(lane):
+        return pltpu.make_async_remote_copy(
+            src_ref=acc.at[other * lanes + lane], dst_ref=xbuf.at[lane],
+            send_sem=xsem.at[0, lane], recv_sem=xsem.at[1, lane],
+            device_id={"col": other}, device_id_type=MESH,
+        )
+
+    def pcopy(lane, step, source):
         peer = lax.rem(row + step, n)
         where = row if source else lax.rem(row + n - step, n)
-        dst = gbuf.at[:, pl.ds(pl.multiple_of(where * left, left), left), :]
-        return pltpu.make_async_remote_copy(
-            src_ref=psend.at[peer], dst_ref=dst, send_sem=psem_s.at[step], recv_sem=psem_r.at[step],
+        dst = gbuf.at[lane, :, pl.ds(pl.multiple_of(where * left, left), left), :]
+        return pltpu.make_async_remote_copy(
+            src_ref=psend.at[lane, peer], dst_ref=dst,
+            send_sem=psem_s.at[lane, step], recv_sem=psem_r.at[lane, step],
             device_id={"row": peer}, device_id_type=MESH,
         )
 
-    def pown():
-        dst = gbuf.at[:, pl.ds(pl.multiple_of(row * left, left), left), :]
-        return pltpu.make_async_copy(psend.at[row], dst, psem_r.at[0])
-
-    for step in list(range(1, n)) + [0]:
-        peer = lax.rem(row + step, n)
-
-        @pl.loop(0, sblk)
-        def _(j):
-            rows = pl.ds(peer * sblk + j, left, stride=d2)
-            for lane in range(lanes):
+    def pown(lane):
+        dst = gbuf.at[lane, :, pl.ds(pl.multiple_of(row * left, left), left), :]
+        return pltpu.make_async_copy(psend.at[lane, row], dst, psem_r.at[lane, 0])
+
+    for lane in range(lanes):
+        pair(lane).start()
+    for lane in range(lanes):
+        pair(lane).wait_recv()
+        for step in list(range(1, n)) + [0]:
+            peer = lax.rem(row + step, n)
+
+            @pl.loop(0, sblk)
+            def _(j):
+                rows = pl.ds(peer * sblk + j, left, stride=d2)
                 value = acc[col * lanes + lane, rows, :] + xbuf[lane, rows, :]
-                psend[peer, j, :, lane * 128:(lane + 1) * 128] = value.astype(jnp.bfloat16)
-
-        if step > 0:
-            pcopy(step, True).start()
-        else:
-            pown().start()
-
-    pown().wait()
-    for step in range(1, n):
-        pcopy(step, False).wait_recv()
+                psend[lane, peer, j] = value.astype(jnp.bfloat16)
+
+            if step > 0:
+                pcopy(lane, step, True).start()
+            else:
+                pown(lane).start()
+
     apair(other).wait_recv()
 
     rows_half = n // 2
@@ -232,25 +234,31 @@
         return jnp.logical_and(col * rows_half + j == row, col == h)
 
     groups = sblk // GROUP
-    for g in range(groups):
-        for e in range(GROUP):
-            at = g * GROUP + e
-            for h in range(2):
-                value = lax.dot_general(
-                    gbuf[at], abuf[h, at], (((0,), (0,)), ((), ())), preferred_element_type=jnp.float32
-                )
-                msend[h, at] = (value * scale).astype(jnp.bfloat16)
-        for j in range(rows_half):
-            for h in range(2):
-                same = is_self(j, h)
-
-                @pl.when(same)
-                def _():
-                    mown(g, j, h).start()
-
-                @pl.when(jnp.logical_not(same))
-                def _():
-                    mcopy(g, j, h).start()
+    each = 128 // cblk
+    for lane in range(lanes):
+        pown(lane).wait()
+        for step in range(1, n):
+            pcopy(lane, step, False).wait_recv()
+        for g in range(groups):
+            for e in range(GROUP):
+                at = g * GROUP + e
+                for h in range(2):
+                    value = lax.dot_general(
+                        gbuf[lane, at], abuf[h, at], (((0,), (0,)), ((), ())),
+                        preferred_element_type=jnp.float32,
+                    )
+                    msend[h, at, lane * 128:(lane + 1) * 128, :] = (value * scale).astype(jnp.bfloat16)
+            for j in range(lane * each, (lane + 1) * each):
+                for h in range(2):
+                    same = is_self(j, h)
+
+                    @pl.when(same)
+                    def _():
+                        mown(g, j, h).start()
+
+                    @pl.when(jnp.logical_not(same))
+                    def _():
+                        mcopy(g, j, h).start()
 
     from_col = row // rows_half
     for g in range(groups):
@@ -282,9 +290,11 @@
 
     for step in range(1, n):
         acopy(step, True).wait_send()
-        pcopy(step, True).wait_send()
+        for lane in range(lanes):
+            pcopy(lane, step, True).wait_send()
     apair(col).wait_send()
-    pair.wait_send()
+    for lane in range(lanes):
+        pair(lane).wait_send()
 
 
 def per_device(half_system, vectors, edge, ket, bra):
@@ -295,7 +305,7 @@
     fits = (
         lax.axis_size("col") == 2 and n % 2 == 0 and d2 % n == 0 and width % n == 0
         and left % 16 == 0 and cblk % 16 == 0 and sblk % GROUP == 0 and kb % (256 * SUBS) == 0
-        and width % 256 == 0 and right % 128 == 0
+        and width % 256 == 0 and 128 % cblk == 0 and right % 128 == 0
     )
     if not fits:
         return plain(half_system, vectors, edge, ket, bra)
@@ -319,8 +329,8 @@
             pltpu.VMEM((2 * SUBS, hrows, piece), bf16),
             pltpu.VMEM((2 * lanes, hrows, 128), f32),
             pltpu.VMEM((lanes, hrows, 128), f32),
-            pltpu.VMEM((n, sblk, left, half), bf16),
-            pltpu.VMEM((sblk, n * left, half), bf16),
+            pltpu.VMEM((lanes, n, sblk, left, 128), bf16),
+            pltpu.VMEM((lanes, sblk, n * left, 128), bf16),
             pltpu.VMEM((2, sblk, n * left, right), bf16),
             pltpu.VMEM((2, sblk, half, right), bf16),
             dma((2, SUBS)),
@@ -329,9 +339,9 @@
             dma((2, n - 1, SUBS)),
             dma((n + 1,)),
             dma((n + 1,)),
-            dma((2,)),
-            dma((n,)),
-            dma((n,)),
+            dma((2, lanes)),
+            dma((lanes, n)),
+            dma((lanes, n)),
             dma((sblk // GROUP, n // 2, 2)),
             dma((sblk // GROUP, n)),
         ],

time: 275 us -> 268 us (0.975)
  Pallas kernels: 267 us -> 258 us
    pallas_call x1, Pallas kernels: 267 us -> 258 us  [per_device(): pl.pallas_call(functools.partial(kernel, n, left, sblk, cblk, float((n *...]
where the time goes in v3:
time: 268 us; the launch traced here: 266 us
  Pallas kernels  258 us (96%)
  matrix products  6.01 us (2%)
    pallas_call x1, Pallas kernels, per_device(): pl.pallas_call(functools.partial(kernel, n, left, sblk, cblk, float((n *...  258 us

profile of v3, /device:TPU:13, one launch (start us, length us, event | category | flops | bytes accessed | tf_op | source)
XLA Modules:
  0.0 265.9 jit_solution(7177381272330504863)
XLA Ops:
  0.0 0.0 copy-start
  0.0 0.9 fusion.4
  0.9 0.3 copy-done
  1.3 0.5 convolution_convert_fusion
  1.7 1.6 copy.7
  3.3 258.0 %renormalize.1 = bf16[64,64,256]{2,1,0:T(8,128)(2,1)} custom-call(bf16[2048,16384]{1,0:T(8,128)(2,1)} %half_ref.1, bf16[2048,512]{1,0:T(8,128)(2,1)} %vec_ref.1, bf16[8,8,32,256]{3,2,1,0:T(8,128)(2,1)} %bitcast.11), custom_call_target="tpu_custom_call" | custom-call | tf_op jit(solution)/shard_map/renormalize/pallas_call | solution.py:322
  261.3 4.6 %convert_bitcast_fusion = bf16[64,64,256]{2,1,0:T(8,128)(2,1)} fusion(bf16[64,64,1]{1,0,2:T(8,128)(2,1)S(1)} %fusion.4, bf16[64,64,256]{2,1,0:T(8,128)(2,1)} %renormalize.1), kind=kOutput, calls=%fused_computation.2 | convolution fusion | flops 135266304 | bytes 4202496 | tf_op jit(solution)/shard_map/ts,scb->ctb/dot_general | solution.py:353
Async XLA Ops:
  0.0 1.3 copy-start
